TPU v7x, 32 devices: a whole 2x2x4 slice. The times are simulated.
32 devices in a mesh: dp: 4 (over z), seq: 8 (over y, x, core).
Axes of the slice: x: 2, y: 2, z: 4, core: 2. Of those that a mesh axis runs over, the one named last changes fastest.
Arguments:
- slide_tiles: bfloat16 [64, 256, 384], P(('dp', 'seq')), parts along dimension 0, may hold values from -6 to 6
- norm_gain: float32 [2, 384], replicated, may hold values from 0.1 to 1.9
- in_weight: bfloat16 [2, 384, 1536], replicated, may hold values from -0.3125 to 0.3125
- state_weight: bfloat16 [2, 384, 44], replicated, may hold values from -0.3125 to 0.3125
- conv_weight: float32 [2, 4, 800], replicated, may hold values from -2.5 to 2.5
- conv_bias: float32 [2, 800], replicated, may hold values from -0.5 to 0.5
- step_bias: float32 [2, 12], replicated, may hold values from -5 to -3
- decay_log: float32 [2, 12], replicated, may hold values from -8.5 to 1
- skip_gain: float32 [2, 12], replicated, may hold values from 0.5 to 1.5
- out_gain: float32 [2, 768], replicated, may hold values from 0.1 to 1.9
- out_weight: bfloat16 [2, 768, 384], replicated, may hold values from -0.21875 to 0.21875
Outputs:
- tile_out: bfloat16 [64, 256, 384], P(('dp', 'seq')), parts along dimension 0
There are 4 independent parts, one for each index of `dp`. A program takes and returns all parts, laid end to end along the dimension named above; an argument that names none is the same for every part. Nothing has to cross between parts.
All inputs are finite; a program needn't handle non-finite values.
Results may differ from a plain program's by a relative error of at most 0.014.
Values may be sent and summed in bfloat16 or wider, within the bound.
A program may use at most 64 MiB of HBM per device.

v0:
```python
import jax
import jax.numpy as jnp
from jax import lax
from jax.sharding import PartitionSpec as P

HEADS = 12
HEADDIM = 64
STATE = 16
GROUP = 256


epsilon = 1e-05


def entering_2(x, axis, join, neutral):
    place = lax.axis_index(axis)
    gathered = jax.tree.map(
        lambda a, kind: lax.all_gather(a.astype(kind), axis), x, (jnp.bfloat16, jnp.bfloat16)
    )
    state = jax.tree.map(lambda a, e: jnp.zeros_like(a) + jnp.asarray(e, a.dtype), x, neutral)

    def one(step, state):
        return join(
            state,
            jax.tree.map(
                lambda a, own: lax.dynamic_index_in_dim(a, step, 0, False).astype(own.dtype),
                gathered,
                x,
            ),
        )

    return lax.fori_loop(0, place, one, state)


def passed_along(value, axis, steps):
    count = lax.axis_size(axis)
    first, last = (max(0, -steps), min(count, count - steps))
    return lax.ppermute(value, axis, [(source, source + steps) for source in range(first, last)])


def rms_scaled(values, scale_gain):
    values = values.astype(jnp.float32)
    return (
        values * lax.rsqrt(jnp.mean(values * values, axis=-1, keepdims=True) + epsilon) * scale_gain
    )


def group_terms(group_in):
    group_x, group_b, group_c, group_step, group_rate = group_in
    cumulative = jnp.cumsum(group_rate, axis=0)
    positions = jnp.arange(group_x.shape[0])
    lower_mask = positions[:, None] >= positions[None, :]
    cum_heads = cumulative.T
    differences = cum_heads[:, :, None] - cum_heads[:, None, :]
    decay_mask = jnp.exp(jnp.where(lower_mask[None], differences, -jnp.inf))
    scores = jnp.dot(group_c, group_b.T, preferred_element_type=jnp.float32)
    weights = (scores[None] * decay_mask * group_step.T[:, None, :]).astype(jnp.bfloat16)
    intra_out = jnp.einsum("hts,shp->thp", weights, group_x, preferred_element_type=jnp.float32)
    tail_weight = jnp.exp(cumulative[-1][None, :] - cumulative) * group_step
    weighted_x = (group_x.astype(jnp.float32) * tail_weight[:, :, None]).astype(jnp.bfloat16)
    local_state = jnp.einsum("shp,sn->hpn", weighted_x, group_b, preferred_element_type=jnp.float32)
    return (intra_out, local_state, cumulative)


def link_states(earlier, latter):
    return (earlier[0] + latter[0], jnp.exp(latter[0])[:, None, None] * earlier[1] + latter[1])


def incoming_state(whole_decay, final_state):
    identity = (jnp.zeros_like(whole_decay), jnp.zeros_like(final_state))
    passed = entering_2((whole_decay, final_state), "seq", link_states, identity)
    return passed[1]


def advance(carry_state, group_item):
    group_total, local_state = group_item
    return (jnp.exp(group_total)[:, None, None] * carry_state + local_state, carry_state)


def mixer(
    sequence,
    layer,
    norm_gain,
    in_weight,
    state_weight,
    conv_weight,
    conv_bias,
    step_bias,
    decay_log,
    skip_gain,
    out_gain,
):
    length = sequence.shape[0]
    inner_width = in_weight.shape[2] // 2
    normed = rms_scaled(sequence, norm_gain[layer]).astype(jnp.bfloat16)
    gate_x = jnp.dot(normed, in_weight[layer], preferred_element_type=jnp.float32).astype(
        jnp.bfloat16
    )
    state_proj = jnp.dot(normed, state_weight[layer], preferred_element_type=jnp.float32).astype(
        jnp.bfloat16
    )
    x_part = gate_x[:, inner_width:]
    bc_part = state_proj[:, : 2 * STATE]
    margin = conv_weight.shape[1] - 1
    edge_rows = passed_along((x_part[length - margin :], bc_part[length - margin :]), "seq", 1)
    x_padded = jnp.concatenate([edge_rows[0], x_part], axis=0)
    bc_padded = jnp.concatenate([edge_rows[1], bc_part], axis=0)
    taps = conv_weight[layer]
    conv_x = jnp.zeros((length, inner_width), jnp.float32) + conv_bias[layer][None, :inner_width]
    conv_bc = jnp.zeros((length, 2 * STATE), jnp.float32) + conv_bias[layer][None, inner_width:]
    for offset in range(margin + 1):
        conv_x = conv_x + taps[offset][None, :inner_width] * x_padded[
            offset : offset + length
        ].astype(jnp.float32)
        conv_bc = conv_bc + taps[offset][None, inner_width:] * bc_padded[
            offset : offset + length
        ].astype(jnp.float32)
    x_conv = jax.nn.silu(conv_x).astype(jnp.bfloat16)
    bc_conv = jax.nn.silu(conv_bc).astype(jnp.bfloat16)
    step_size = jax.nn.softplus(
        state_proj[:, 2 * STATE :].astype(jnp.float32) + step_bias[layer][None, :]
    )
    log_rates = -step_size * jnp.exp(decay_log[layer])[None, :]
    group_count = length // GROUP
    group_x = x_conv.reshape(group_count, GROUP, HEADS, HEADDIM)
    group_c = bc_conv[:, STATE:].reshape(group_count, GROUP, STATE)
    inputs = (
        group_x,
        bc_conv[:, :STATE].reshape(group_count, GROUP, STATE),
        group_c,
        step_size.reshape(group_count, GROUP, HEADS),
        log_rates.reshape(group_count, GROUP, HEADS),
    )
    intra_out, local_states, cumulative = lax.map(group_terms, inputs)
    totals = cumulative[:, -1, :]
    final_state, entering = lax.scan(
        advance, jnp.zeros((HEADS, HEADDIM, STATE), jnp.float32), (totals, local_states)
    )
    arriving = incoming_state(jnp.sum(totals, axis=0), final_state)
    before = jnp.cumsum(totals, axis=0) - totals
    start_states = entering + jnp.exp(before)[:, :, None, None] * arriving[None]
    inter_out = jnp.exp(cumulative)[..., None] * jnp.einsum(
        "ctn,chpn->cthp", group_c.astype(jnp.float32), start_states, precision=lax.Precision.HIGHEST
    )
    y_total = (
        intra_out + inter_out + skip_gain[layer][None, None, :, None] * group_x.astype(jnp.float32)
    )
    gated = y_total.reshape(length, inner_width) * jax.nn.silu(
        gate_x[:, :inner_width].astype(jnp.float32)
    )
    return rms_scaled(gated, out_gain[layer]).astype(jnp.bfloat16)


def on_device(
    slide_tiles,
    norm_gain,
    in_weight,
    state_weight,
    conv_weight,
    conv_bias,
    step_bias,
    decay_log,
    skip_gain,
    out_gain,
    out_weight,
):
    row_count, col_count, feature_count = slide_tiles.shape
    params = (
        norm_gain,
        in_weight,
        state_weight,
        conv_weight,
        conv_bias,
        step_bias,
        decay_log,
        skip_gain,
        out_gain,
    )
    flipped = slide_tiles[:, ::-1, :]
    columns = lax.all_to_all(flipped, "seq", split_axis=1, concat_axis=0, tiled=True)
    full_rows, block_cols = (columns.shape[0], columns.shape[1])
    first_order = jnp.transpose(columns[::-1], (1, 0, 2)).reshape(
        full_rows * block_cols, feature_count
    )
    mixed_out = mixer(first_order, 0, *params)
    layer_out = (
        first_order.astype(jnp.float32)
        + jnp.dot(mixed_out, out_weight[0], preferred_element_type=jnp.float32)
    ).astype(jnp.bfloat16)
    row_grid = jnp.transpose(layer_out.reshape(block_cols, full_rows, feature_count), (1, 0, 2))[
        ::-1
    ]
    returned = lax.all_to_all(row_grid, "seq", split_axis=0, concat_axis=1, tiled=True)
    second = returned[:, ::-1, :].reshape(row_count * col_count, feature_count)
    mixed_out = mixer(second, 1, *params)
    result = (
        second.astype(jnp.float32)
        + jnp.dot(mixed_out, out_weight[1], preferred_element_type=jnp.float32)
    ).astype(jnp.bfloat16)
    return result.reshape(row_count, col_count, feature_count)


def solution(mesh):
    placed = (P(("dp", "seq"), None, None), P(), P(), P(), P(), P(), P(), P(), P(), P(), P())
    return jax.shard_map(
        on_device,
        mesh=mesh,
        in_specs=placed,
        out_specs=P(("dp", "seq"), None, None),
        check_vma=False,
    )
```

profile of v0, /device:TPU:0, one launch (start us, length us, event | category | flops | bytes accessed | tf_op | source)
XLA Modules:
  0.0 138.6 jit_solution(18102543792137817311)
XLA Ops:
  0.1 1.5 %copy.98 = bf16[2,256,384]{2,0,1:T(2,128)(2,1)S(1)} copy(bf16[2,256,384]{2,1,0:T(8,128)(2,1)} %param.23) | data formatting | bytes 786432 | tf_op args[0]
  1.5 1.0 rev.12
  2.5 5.2 %all-to-all-start = ((bf16[2,256,384]{2,0,1:T(2,128)(2,1)}), bf16[2,256,384]{2,0,1:T(2,128)(2,1)S(1)}, u32[]{:S(2)}, u32[]{:S(2)}) async-start(bf16[2,256,384]{2,0,1:T(2,128)(2,1)} %rev.12), calls=%async_computation | async-start | bytes 786432 | tf_op jit(solution)/shard_map/all_to_all | solution.py:180
  13.0 0.6 slice_reduce_fusion.12
  13.6 0.7 fusion.105
  14.3 1.7 %all-to-all-done = bf16[2,256,384]{2,0,1:T(2,128)(2,1)S(1)} async-done(((bf16[2,256,384]{2,0,1:T(2,128)(2,1)}), bf16[2,256,384]{2,0,1:T(2,128)(2,1)S(1)}, u32[]{:S(2)}, u32[]{:S(2)}) %all-to-all-start) | async-done | bytes 393248 | tf_op jit(solution)/shard_map/all_to_all | solution.py:180
  17.5 2.3 %convolution_convert_fusion.1 = bf16[512,1536]{1,0:T(8,128)(2,1)S(1)} fusion(bf16[512,384]{1,0:T(8,128)(2,1)S(1)} %bitcast.348, bf16[2,384,1536]{2,1,0:T(8,128)(2,1)} %param.25), kind=kOutput, calls=%fused_computation.95 | convolution fusion | flops 604766208 | bytes 3145728 | tf_op jit(solution)/shard_map/dot_general | solution.py:96
  19.8 1.0 convert_element_type.292
  21.1 1.3 collective-permute-start.1
  22.4 3.2 %collective-permute-start = (bf16[3,768]{1,0:T(4,128)(2,1)S(1)}, bf16[3,768]{1,0:T(4,128)(2,1)S(1)}, u32[]{:S(2)}, u32[]{:S(2)}) collective-permute-start(bf16[3,768]{1,0:T(4,128)(2,1)S(1)} %slice.368), channel_id=1, source_target_pairs={{0,1},{1,2},{2,3},{3,4},{4,5},{5,6},{6,7},{8,9},{9,10},{10,11},{11... | collective-permute-start | bytes 13832 | tf_op jit(solution)/shard_map/ppermute | solution.py:38
  26.0 0.6 reshape.377
  26.6 1.1 multiply_convert_fusion.17
  28.5 0.6 broadcast.140.clone
  29.1 8.0 %while.78 = (s32[]{:T(128)}, f32[2,256,12,64]{1,3,2,0:T(8,128)S(1)}, f32[2,12,64,16]{2,3,1,0:T(8,128)S(1)}, f32[2,256,12]{1,2,0:T(8,128)}, bf16[2,256,12,64]{1,3...) while((s32[]{:T(128)}, ...), condition=%wide.region_4.5_spmd, body=%wide.region_1.4_spmd.sunk | while | flops 114038824 | bytes 2966549 | solution.py:134
  30.9 1.0 fusion.138
  32.4 0.6 bitcast_dynamic-update-slice_fusion.8
  34.9 1.0 fusion.138
  36.4 0.6 bitcast_dynamic-update-slice_fusion.8
  37.0 1.0 slice_reduce_fusion.6
  38.0 0.8 exp.113
  39.2 10.9 %all-gather.1 = bf16[96,64,16]{1,2,0:T(8,128)(2,1)S(1)} all-gather(bf16[12,64,16]{1,2,0:T(8,128)(2,1)S(1)} %convert_element_type.257), channel_id=3, replica_groups=mesh['dp'=4,'seq'=8] {'seq'}, dimensions={0}, use_global_device_ids=true | all-gather | bytes 221184 | tf_op jit(solution)/shard_map/all_gather | solution.py:18
  50.3 13.2 %all-reduce = bf16[96]{0:T(256)(128)(2,1)S(1)} all-reduce(bf16[96]{0:T(256)(128)(2,1)S(1)} %dynamic-update-slice), channel_id=2, replica_groups=mesh['dp'=4,'seq'=8] {'seq'}, use_global_device_ids=true, to_apply=%add | all-reduce | flops 96 | bytes 384
  63.9 1.3 multiply_add_fusion.1
  65.2 1.2 copy.109
  67.1 1.9 %multiply_reduce_fusion.1 = f32[512]{0:T(512)S(1)} fusion(f32[512,768]{1,0:T(8,128)S(1)} %copy.110, bf16[512,1536]{1,0:T(8,128)(2,1)} %copy-done.4), kind=kLoop, calls=%fused_computation.113 | loop fusion | flops 3145216 | bytes 2361344 | tf_op jit(solution)/shard_map/reduce_sum | solution.py:44
  68.9 1.9 %fusion.68 = bf16[512,384]{1,0:T(8,128)(2,1)S(1)} fusion(f32[512,384]{1,0:T(8,128)S(1)} %bitcast.351, f32[768]{0:T(1024)S(1)} %copy-done.25, f32[512]{0:T(512)S(1)} %add_rsqrt_fusion.3, bf16[2,768,384]{2,1,0:T(8,128)(2,1)} %param.33, f32[512,768]{1,0:T(8,128)S(1)} %copy.110, bf16[512,1536]{1,0:T(8,128)(2,1)S(1)} %copy-done.5), kind=kOutput, calls=%fused_computation.118 | convolution fusion | flops 305922048 | bytes 4134912 | tf_op jit(solution)/shard_map/dot_general | solution.py:188
  70.9 0.8 rev.14
  71.7 3.6 %all-to-all-start.1 = ((bf16[16,32,384]{2,1,0:T(8,128)(2,1)}), bf16[16,32,384]{2,1,0:T(8,128)(2,1)S(1)}, u32[]{:S(2)}, u32[]{:S(2)}) async-start(bf16[16,32,384]{2,1,0:T(8,128)(2,1)} %rev.14), calls=%async_computation.1 | async-start | bytes 786432 | tf_op jit(solution)/shard_map/all_to_all | solution.py:193
  75.3 8.2 %all-to-all-done.1 = bf16[16,32,384]{2,1,0:T(8,128)(2,1)S(1)} async-done(((bf16[16,32,384]{2,1,0:T(8,128)(2,1)}), bf16[16,32,384]{2,1,0:T(8,128)(2,1)S(1)}, u32[]{:S(2)}, u32[]{:S(2)}) %all-to-all-start.1) | async-done | bytes 393248 | tf_op jit(solution)/shard_map/all_to_all | solution.py:193
  84.8 2.3 %convolution_convert_fusion = bf16[512,1536]{1,0:T(8,128)(2,1)S(1)} fusion(bf16[512,384]{1,0:T(8,128)(2,1)S(1)} %bitcast.346, bf16[2,384,1536]{2,1,0:T(8,128)(2,1)} %param.25), kind=kOutput, calls=%fused_computation.94 | convolution fusion | flops 604766208 | bytes 3145728 | tf_op jit(solution)/shard_map/dot_general | solution.py:96
  87.2 1.0 copy-done.2
  88.2 1.3 collective-permute-start.3
  89.5 3.2 %collective-permute-start.2 = (bf16[3,768]{1,0:T(4,128)(2,1)S(1)}, bf16[3,768]{1,0:T(4,128)(2,1)S(1)}, u32[]{:S(2)}, u32[]{:S(2)}) collective-permute-start(bf16[3,768]{1,0:T(4,128)(2,1)S(1)} %slice.384), channel_id=1, source_target_pairs={{0,1},{1,2},{2,3},{3,4},{4,5},{5,6},{6,7},{8,9},{9,10},{10,11},{11... | collective-permute-start | bytes 13832 | tf_op jit(solution)/shard_map/ppermute | solution.py:38
  93.1 0.6 reshape.384
  93.7 1.1 multiply_convert_fusion.15
  96.2 7.9 %while.80 = (s32[]{:T(128)}, f32[2,256,12,64]{1,3,2,0:T(8,128)S(1)}, f32[2,12,64,16]{2,3,1,0:T(8,128)S(1)}, f32[2,256,12]{1,2,0:T(8,128)}, bf16[2,256,12,64]{1,3...) while((s32[]{:T(128)}, ...), condition=%wide.region_16.17_spmd, body=%wide.region_13.16_spmd.sunk | while | flops 114038824 | bytes 2966549 | solution.py:134
  98.0 1.0 fusion.147
  99.6 0.6 bitcast_dynamic-update-slice_fusion.9
  102.0 1.0 fusion.147
  103.5 0.6 bitcast_dynamic-update-slice_fusion.9
  104.1 1.0 slice_reduce_fusion.4
  105.1 0.8 exp.120
  106.3 10.8 %all-gather.3 = bf16[96,64,16]{1,2,0:T(8,128)(2,1)S(1)} all-gather(bf16[12,64,16]{1,2,0:T(8,128)(2,1)S(1)} %convert_element_type.282), channel_id=5, replica_groups=mesh['dp'=4,'seq'=8] {'seq'}, dimensions={0}, use_global_device_ids=true | all-gather | bytes 221184 | tf_op jit(solution)/shard_map/all_gather | solution.py:18
  117.3 13.2 %all-reduce.1 = bf16[96]{0:T(256)(128)(2,1)S(1)} all-reduce(bf16[96]{0:T(256)(128)(2,1)S(1)} %dynamic-update-slice.1), channel_id=4, replica_groups=mesh['dp'=4,'seq'=8] {'seq'}, use_global_device_ids=true, to_apply=%add.1 | all-reduce | flops 96 | bytes 384
  130.9 1.3 multiply_add_fusion
  132.2 1.2 copy.122
  134.1 1.8 %multiply_reduce_fusion = f32[512]{0:T(512)S(1)} fusion(f32[512,768]{1,0:T(8,128)S(1)} %copy.123, bf16[512,1536]{1,0:T(8,128)(2,1)} %copy-done.2), kind=kLoop, calls=%fused_computation.109 | loop fusion | flops 3145216 | bytes 2361344 | tf_op jit(solution)/shard_map/reduce_sum | solution.py:44
  136.0 2.6 %fusion.69 = bf16[512,384]{1,0:T(8,128)(2,1)} fusion(f32[768]{0:T(1024)S(1)} %copy-done.24, f32[512]{0:T(512)S(1)} %add_rsqrt_fusion.1, bf16[2,768,384]{2,1,0:T(8,128)(2,1)} %param.33, f32[512,768]{1,0:T(8,128)S(1)} %copy.123, bf16[512,1536]{1,0:T(8,128)(2,1)S(1)} %copy-done.3, bf16[512,384]{1,0:T(8,128)(2,1)S(1)} %bitcast.336), kind=kOutput, calls=%fused_computation.119 | convolution fusion | flops 306118656 | bytes 3741696 | tf_op jit(solution)/shard_map/dot_general | solution.py:198
  (257 shorter events, 23.0 us)
Async XLA Ops:
  0.0 11.8 %copy-start.39 = (u32[32]{0:T(128)S(1)}, u32[32]{0:T(128)}, u32[]{:S(2)}) copy-start(u32[32]{0:T(128)} %constant.128) | copy-start | bytes 388
  0.0 7.7 %copy-start.22 = (f32[2,800]{1,0:T(2,128)S(1)}, f32[2,800]{1,0:T(2,128)}, u32[]{:S(2)}) copy-start(f32[2,800]{1,0:T(2,128)} %param.28) | copy-start | bytes 19204
  0.0 8.9 %copy-start.26 = (f32[2,384]{1,0:T(2,128)S(1)}, f32[2,384]{1,0:T(2,128)}, u32[]{:S(2)}) copy-start(f32[2,384]{1,0:T(2,128)} %param.24) | copy-start | bytes 9220
  0.0 9.5 %copy-start.15 = (f32[2,4,800]{2,1,0:T(4,128)S(1)}, f32[2,4,800]{2,1,0:T(4,128)}, u32[]{:S(2)}) copy-start(f32[2,4,800]{2,1,0:T(4,128)} %param.27) | copy-start | bytes 76804
  0.0 10.1 %copy-start.36 = (f32[2,12]{1,0:T(2,128)S(1)}, f32[2,12]{1,0:T(2,128)}, u32[]{:S(2)}) copy-start(f32[2,12]{1,0:T(2,128)} %param.31) | copy-start | bytes 292
  0.0 10.6 %copy-start.23 = (f32[2,768]{1,0:T(2,128)S(1)}, f32[2,768]{1,0:T(2,128)}, u32[]{:S(2)}) copy-start(f32[2,768]{1,0:T(2,128)} %param.32) | copy-start | bytes 18436
  0.0 11.2 %copy-start.38 = (f32[2,12]{1,0:T(2,128)S(1)}, f32[2,12]{1,0:T(2,128)}, u32[]{:S(2)}) copy-start(f32[2,12]{1,0:T(2,128)} %param.29) | copy-start | bytes 292
  0.0 11.2 %copy-start.37 = (f32[2,12]{1,0:T(2,128)S(1)}, f32[2,12]{1,0:T(2,128)}, u32[]{:S(2)}) copy-start(f32[2,12]{1,0:T(2,128)} %param.30) | copy-start | bytes 292
  0.0 13.6 %copy-start.11 = (bf16[2,384,44]{1,0,2:T(2,128)(2,1)S(1)}, bf16[2,384,44]{1,0,2:T(2,128)(2,1)}, u32[]{:S(2)}) copy-start(bf16[2,384,44]{1,0,2:T(2,128)(2,1)} %param.26) | copy-start | bytes 202756
  2.5 13.5 %all-to-all-start = ((bf16[2,256,384]{2,0,1:T(2,128)(2,1)}), bf16[2,256,384]{2,0,1:T(2,128)(2,1)S(1)}, u32[]{:S(2)}, u32[]{:S(2)}) async-start(bf16[2,256,384]{2,0,1:T(2,128)(2,1)} %rev.12), calls=%async_computation | async-start | bytes 786432 | tf_op jit(solution)/shard_map/all_to_all | solution.py:180
  19.7 1.4 %copy-start.4 = (bf16[512,1536]{1,0:T(8,128)(2,1)}, bf16[512,1536]{1,0:T(8,128)(2,1)S(1)}, u32[]{:S(2)}) copy-start(bf16[512,1536]{1,0:T(8,128)(2,1)S(1)} %convolution_convert_fusion.1) | copy-start | bytes 4718596
  21.1 4.6 %collective-permute-start.1 = (bf16[3,32]{0,1:T(8,128)(2,1)S(1)}, bf16[3,32]{0,1:T(8,128)(2,1)S(1)}, u32[]{:S(2)}, u32[]{:S(2)}) collective-permute-start(bf16[3,32]{0,1:T(8,128)(2,1)S(1)} %slice.374), channel_id=1, source_target_pairs={{0,1},{1,2},{2,3},{3,4},{4,5},{5,6},{6,7},{8,9},{9,10},{10,11},{11... | collective-permute-start | bytes 584 | tf_op jit(solution)/shard_map/ppermute | solution.py:38
  22.4 4.2 %collective-permute-start = (bf16[3,768]{1,0:T(4,128)(2,1)S(1)}, bf16[3,768]{1,0:T(4,128)(2,1)S(1)}, u32[]{:S(2)}, u32[]{:S(2)}) collective-permute-start(bf16[3,768]{1,0:T(4,128)(2,1)S(1)} %slice.368), channel_id=1, source_target_pairs={{0,1},{1,2},{2,3},{3,4},{4,5},{5,6},{6,7},{8,9},{9,10},{10,11},{11... | collective-permute-start | bytes 13832 | tf_op jit(solution)/shard_map/ppermute | solution.py:38
  29.1 0.6 copy-start.9
  30.9 2.2 %copy-start.10 = (f32[2,256,12]{1,0,2:T(2,128)S(1)}, f32[2,256,12]{1,0,2:T(2,128)}, u32[]{:S(2)}) copy-start(f32[2,256,12]{1,0,2:T(2,128)} %copy-done.9) | copy-start | bytes 73732 | tf_op jit(solution)/shard_map/while
  33.0 0.6 copy-start.9
  34.9 2.2 %copy-start.10 = (f32[2,256,12]{1,0,2:T(2,128)S(1)}, f32[2,256,12]{1,0,2:T(2,128)}, u32[]{:S(2)}) copy-start(f32[2,256,12]{1,0,2:T(2,128)} %copy-done.9) | copy-start | bytes 73732 | tf_op jit(solution)/shard_map/while
  39.2 24.7 %copy-start.14 = (bf16[2,256,16]{1,0,2:T(2,128)(2,1)S(1)}, bf16[2,256,16]{1,0,2:T(2,128)(2,1)}, u32[]{:S(2)}) copy-start(bf16[2,256,16]{1,0,2:T(2,128)(2,1)} %reshape.377) | copy-start | bytes 49156
  39.2 24.7 %copy-start.33 = (f32[12]{0:T(128)S(1)}, f32[12]{0:T(128)}, u32[]{:S(2)}) copy-start(f32[12]{0:T(128)} %get-tuple-element.486) | copy-start | bytes 148
  67.0 1.9 %copy-start.5 = (bf16[512,1536]{1,0:T(8,128)(2,1)S(1)}, bf16[512,1536]{1,0:T(8,128)(2,1)}, u32[]{:S(2)}) copy-start(bf16[512,1536]{1,0:T(8,128)(2,1)} %copy-done.4) | copy-start | bytes 4718596
  67.0 1.9 %copy-start.6 = (f32[16,32,384]{2,0,1:T(8,128)S(1)}, f32[16,32,384]{2,0,1:T(8,128)}, u32[]{:S(2)}) copy-start(f32[16,32,384]{2,0,1:T(8,128)} %convert_element_type.292) | copy-start | bytes 2359300
  67.0 1.9 %copy-start.25 = (f32[768]{0:T(1024)S(1)}, f32[768]{0:T(1024)}, u32[]{:S(2)}) copy-start(f32[768]{0:T(1024)} %get-tuple-element.382) | copy-start | bytes 9220
  71.7 12.6 %copy-start.21 = (f32[384]{0:T(512)S(1)}, f32[384]{0:T(512)}, u32[]{:S(2)}) copy-start(f32[384]{0:T(512)} %get-tuple-element.383) | copy-start | bytes 4612
  71.7 11.8 %all-to-all-start.1 = ((bf16[16,32,384]{2,1,0:T(8,128)(2,1)}), bf16[16,32,384]{2,1,0:T(8,128)(2,1)S(1)}, u32[]{:S(2)}, u32[]{:S(2)}) async-start(bf16[16,32,384]{2,1,0:T(8,128)(2,1)} %rev.14), calls=%async_computation.1 | async-start | bytes 786432 | tf_op jit(solution)/shard_map/all_to_all | solution.py:193
  75.3 9.2 %copy-start.12 = (bf16[1,384,44]{1,0,2:T(2,128)(2,1)S(1)}, bf16[1,384,44]{1,0,2:T(2,128)(2,1)}, u32[]{:S(2)}) copy-start(bf16[1,384,44]{1,0,2:T(2,128)(2,1)} %get-tuple-element.465) | copy-start | bytes 101380
  84.1 3.0 %copy-start = (bf16[2,256,384]{2,1,0:T(8,128)(2,1)}, bf16[2,256,384]{2,1,0:T(8,128)(2,1)S(1)}, u32[]{:S(2)}) copy-start(bf16[2,256,384]{2,1,0:T(8,128)(2,1)S(1)} %rev.15) | copy-start | bytes 1179652
  87.0 1.2 copy-start.2
  87.0 5.6 %copy-start.34 = (f32[12]{0:T(128)S(1)}, f32[12]{0:T(128)}, u32[]{:S(2)}) copy-start(f32[12]{0:T(128)} %get-tuple-element.489) | copy-start | bytes 148
  87.1 5.6 %copy-start.35 = (f32[12]{0:T(128)S(1)}, f32[12]{0:T(128)}, u32[]{:S(2)}) copy-start(f32[12]{0:T(128)} %get-tuple-element.492) | copy-start | bytes 148
  87.1 5.8 %copy-start.27 = (f32[32]{0:T(128)S(1)}, f32[32]{0:T(128)}, u32[]{:S(2)}) copy-start(f32[32]{0:T(128)} %get-tuple-element.475) | copy-start | bytes 388
  87.1 5.8 %copy-start.28 = (f32[32]{0:T(128)S(1)}, f32[32]{0:T(128)}, u32[]{:S(2)}) copy-start(f32[32]{0:T(128)} %get-tuple-element.479) | copy-start | bytes 388
  87.1 5.8 %copy-start.29 = (f32[32]{0:T(128)S(1)}, f32[32]{0:T(128)}, u32[]{:S(2)}) copy-start(f32[32]{0:T(128)} %get-tuple-element.481) | copy-start | bytes 388
  87.1 5.8 %copy-start.30 = (f32[32]{0:T(128)S(1)}, f32[32]{0:T(128)}, u32[]{:S(2)}) copy-start(f32[32]{0:T(128)} %get-tuple-element.482) | copy-start | bytes 388
  87.1 5.8 %copy-start.32 = (f32[32]{0:T(128)S(1)}, f32[32]{0:T(128)}, u32[]{:S(2)}) copy-start(f32[32]{0:T(128)} %get-tuple-element.483) | copy-start | bytes 388
  87.1 6.6 %copy-start.16 = (f32[768]{0:T(1024)S(1)}, f32[768]{0:T(1024)}, u32[]{:S(2)}) copy-start(f32[768]{0:T(1024)} %get-tuple-element.371) | copy-start | bytes 9220
  87.1 6.6 %copy-start.17 = (f32[768]{0:T(1024)S(1)}, f32[768]{0:T(1024)}, u32[]{:S(2)}) copy-start(f32[768]{0:T(1024)} %get-tuple-element.372) | copy-start | bytes 9220
  87.1 6.6 %copy-start.18 = (f32[768]{0:T(1024)S(1)}, f32[768]{0:T(1024)}, u32[]{:S(2)}) copy-start(f32[768]{0:T(1024)} %get-tuple-element.373) | copy-start | bytes 9220
  87.1 6.6 %copy-start.19 = (f32[768]{0:T(1024)S(1)}, f32[768]{0:T(1024)}, u32[]{:S(2)}) copy-start(f32[768]{0:T(1024)} %get-tuple-element.374) | copy-start | bytes 9220
  87.2 6.6 %copy-start.20 = (f32[768]{0:T(1024)S(1)}, f32[768]{0:T(1024)}, u32[]{:S(2)}) copy-start(f32[768]{0:T(1024)} %get-tuple-element.379) | copy-start | bytes 9220
  88.2 4.7 %collective-permute-start.3 = (bf16[3,32]{0,1:T(8,128)(2,1)S(1)}, bf16[3,32]{0,1:T(8,128)(2,1)S(1)}, u32[]{:S(2)}, u32[]{:S(2)}) collective-permute-start(bf16[3,32]{0,1:T(8,128)(2,1)S(1)} %slice.390), channel_id=1, source_target_pairs={{0,1},{1,2},{2,3},{3,4},{4,5},{5,6},{6,7},{8,9},{9,10},{10,11},{11... | collective-permute-start | bytes 584 | tf_op jit(solution)/shard_map/ppermute | solution.py:38
  89.5 4.2 %collective-permute-start.2 = (bf16[3,768]{1,0:T(4,128)(2,1)S(1)}, bf16[3,768]{1,0:T(4,128)(2,1)S(1)}, u32[]{:S(2)}, u32[]{:S(2)}) collective-permute-start(bf16[3,768]{1,0:T(4,128)(2,1)S(1)} %slice.384), channel_id=1, source_target_pairs={{0,1},{1,2},{2,3},{3,4},{4,5},{5,6},{6,7},{8,9},{9,10},{10,11},{11... | collective-permute-start | bytes 13832 | tf_op jit(solution)/shard_map/ppermute | solution.py:38
  98.0 2.1 %copy-start.8 = (f32[2,256,12]{1,0,2:T(2,128)S(1)}, f32[2,256,12]{1,0,2:T(2,128)}, u32[]{:S(2)}) copy-start(f32[2,256,12]{1,0,2:T(2,128)} %copy-done.7) | copy-start | bytes 73732 | tf_op jit(solution)/shard_map/while
  102.0 2.1 %copy-start.8 = (f32[2,256,12]{1,0,2:T(2,128)S(1)}, f32[2,256,12]{1,0,2:T(2,128)}, u32[]{:S(2)}) copy-start(f32[2,256,12]{1,0,2:T(2,128)} %copy-done.7) | copy-start | bytes 73732 | tf_op jit(solution)/shard_map/while
  106.3 24.7 %copy-start.13 = (bf16[2,256,16]{1,0,2:T(2,128)(2,1)S(1)}, bf16[2,256,16]{1,0,2:T(2,128)(2,1)}, u32[]{:S(2)}) copy-start(bf16[2,256,16]{1,0,2:T(2,128)(2,1)} %reshape.384) | copy-start | bytes 49156
  106.3 24.7 %copy-start.31 = (f32[12]{0:T(128)S(1)}, f32[12]{0:T(128)}, u32[]{:S(2)}) copy-start(f32[12]{0:T(128)} %get-tuple-element.485) | copy-start | bytes 148
  134.1 1.9 %copy-start.1 = (bf16[2,256,384]{2,1,0:T(8,128)(2,1)S(1)}, bf16[2,256,384]{2,1,0:T(8,128)(2,1)}, u32[]{:S(2)}) copy-start(bf16[2,256,384]{2,1,0:T(8,128)(2,1)} %copy-done) | copy-start | bytes 1179652
  134.1 1.9 %copy-start.3 = (bf16[512,1536]{1,0:T(8,128)(2,1)S(1)}, bf16[512,1536]{1,0:T(8,128)(2,1)}, u32[]{:S(2)}) copy-start(bf16[512,1536]{1,0:T(8,128)(2,1)} %copy-done.2) | copy-start | bytes 4718596
  134.1 1.9 %copy-start.24 = (f32[768]{0:T(1024)S(1)}, f32[768]{0:T(1024)}, u32[]{:S(2)}) copy-start(f32[768]{0:T(1024)} %get-tuple-element.381) | copy-start | bytes 9220
  (2 other events, 1.2 us)
where the time goes:
time: 140 us; the launch traced here: 139 us
  blocking collectives  48.3 us (34%)
  local copies, waits for them, and re-layouts  28.6 us (20%)
  matrix products  17.9 us (13%)
  starting transfers between devices  17.7 us (13%)
  other arithmetic  13.7 us (10%)
  waiting for transfers between devices  9.95 us (7%)
  between operations  1.55 us (1%)
    unnamed x2, blocking collectives  26.5 us
    all_gather x2, blocking collectives, entering_2(): lax.all_gather(a.astype(kind), axis)  21.8 us
    ppermute x4, starting transfers between devices, passed_along(): lax.ppermute(value, axis, [(source, source + steps) for source in range(f...  8.94 us
    all_to_all x1, waiting for transfers between devices, on_device(): lax.all_to_all(row_grid, 'seq', split_axis=0, concat_axis=1, tiled=True)  8.22 us
    all_to_all x1, starting transfers between devices, on_device(): lax.all_to_all(flipped, 'seq', split_axis=1, concat_axis=0, tiled=True)  5.2 us
    dot_general x2, matrix products, mixer(): jnp.dot(normed, in_weight[layer], preferred_element_type=jnp.float32)  4.51 us
    unnamed x80, local copies, waits for them, and re-layouts  4.07 us
    reduce_sum x4, other arithmetic, rms_scaled(): jnp.mean(values * values, axis=-1, keepdims=True) + epsilon  3.99 us
  transfers between devices with their start and end apart: 6, of which 2 were waited for; matrix products, arithmetic and copies ran while one was open for 6% of the time, Pallas kernels for 0%

commit v1 on v0

v1 whole, which is shorter than its diff:
```python
import functools

import jax
import jax.numpy as jnp
from jax import lax
from jax.experimental import pallas as pl
from jax.experimental.pallas import tpu as pltpu
from jax.sharding import PartitionSpec as P

HEADS = 12
HEADDIM = 64
STATE = 16
GROUP = 256
EDGE = 16
EPS = 1e-05
MESH = pl.DeviceIdType.MESH
F32 = jnp.float32
BF16 = jnp.bfloat16


def silu(v):
    half = 0.5 * v
    return half + half * jnp.tanh(half)


def rms(v, gain):
    return v * lax.rsqrt(jnp.mean(v * v, axis=-1, keepdims=True) + EPS) * gain


def halves(v):
    high = v.astype(BF16)
    low = (v - high.astype(F32)).astype(BF16)
    return jnp.concatenate([high, low], axis=1)


def iota(shape, dim):
    return lax.broadcasted_iota(jnp.int32, shape, dim)


def one_hot(cond):
    return jnp.where(cond, 1.0, 0.0).astype(BF16)


def dot(a, b):
    return jnp.dot(a, b, preferred_element_type=F32)


def kernel(
    n,
    slide,
    norm_gain,
    in_hbm,
    state_weight,
    conv_weight,
    conv_bias,
    step_bias,
    decay_log,
    skip_gain,
    out_gain,
    out_hbm,
    out,
    in_w,
    out_w,
    r1,
    edge1,
    o1,
    r2,
    edge2,
    u_ref,
    x_ref,
    p_ref,
    small,
    z_ref,
    y_ref,
    grow_ref,
    c_ref,
    local_ref,
    send0,
    send1,
    gather0,
    gather1,
    arrive,
    w_sem,
    l_sem,
    s1,
    v1,
    e1s,
    e1r,
    s2,
    v2,
    e2s,
    e2r,
    g0s,
    g0r,
    g1s,
    g1r,
):
    me = lax.axis_index("seq")
    rows, cols, width = slide.shape
    full = rows * n
    block = cols // n
    tokens = rows * cols
    inner = in_hbm.shape[2] // 2
    groups = tokens // GROUP
    taps = conv_weight.shape[1]
    sources, edge = edge1.shape[0] // rows, edge1.shape[1]

    def remote(src, dst, send_sem, recv_sem, to):
        return pltpu.make_async_remote_copy(
            src_ref=src,
            dst_ref=dst,
            send_sem=send_sem,
            recv_sem=recv_sem,
            device_id={"seq": to},
            device_id_type=MESH,
        )

    weights_in = pltpu.make_async_copy(in_hbm, in_w, w_sem.at[0])
    weights_out = pltpu.make_async_copy(out_hbm, out_w, w_sem.at[1])
    weights_in.start()
    weights_out.start()

    barrier = pltpu.get_barrier_semaphore()
    for k in range(1, n):
        pl.semaphore_signal(
            barrier, inc=1, device_id={"seq": lax.rem(me + k, n)}, device_id_type=MESH
        )
    pl.semaphore_wait(barrier, n - 1)

    def at_cols(j):
        return pl.ds(pl.multiple_of(j * block, block), block)

    def at_rows(j):
        return pl.ds(j * rows, rows)

    first_copies = []
    for k in range(1, n):
        to = lax.rem(me + k, n)
        copy = remote(
            slide.at[:, at_cols(to), :], r1.at[at_rows(me)], s1.at[k - 1], v1.at[k - 1], to
        )
        copy.start()
        first_copies.append(copy)
    own = pltpu.make_async_copy(slide.at[:, at_cols(me), :], r1.at[at_rows(me)], l_sem.at[0])
    own.start()

    def edge1_copy(source, j):
        return remote(
            slide.at[:, pl.ds((j + 1) * block, edge), :],
            edge1.at[pl.ds(source * rows, rows)],
            e1s.at[j],
            e1r.at[source],
            j,
        )

    def edge1_own(source):
        return pltpu.make_async_copy(
            slide.at[:, pl.ds((source + 1) * block, edge), :],
            edge1.at[pl.ds(source * rows, rows)],
            l_sem.at[1],
        )

    for source in range(sources):

        @pl.when(me == source)
        def _():
            for j in range(n - 1):
                if j != source:
                    edge1_copy(source, j).start()
            edge1_own(source).start()

    @pl.when(me == n - 1)
    def _():
        edge1[...] = jnp.zeros_like(edge1)

    @pl.when(me == 0)
    def _():
        edge2[...] = jnp.zeros_like(edge2)

    small[...] = jnp.zeros_like(small)
    for layer in range(2):
        small[layer, 0:taps, 0 : 2 * STATE] = conv_weight[layer, :, inner : inner + 2 * STATE]
        small[layer, 4:5, 0 : 2 * STATE] = conv_bias[layer : layer + 1, inner : inner + 2 * STATE]
        small[layer, 5:6, 0:HEADS] = step_bias[layer : layer + 1, :]
        small[layer, 6:7, 0:HEADS] = decay_log[layer : layer + 1, :]
        small[layer, 7:8, 0:HEADS] = skip_gain[layer : layer + 1, :]
    p_ref[...] = jnp.zeros_like(p_ref)

    lanes = 128
    spread_row = iota((2 * lanes, inner), 0)
    spread = one_hot((spread_row % lanes) == (iota((2 * lanes, inner), 1) // HEADDIM))

    own.wait()
    for copy in first_copies:
        copy.wait_recv()
    for source in range(sources):

        @pl.when((me != source) & (me < n - 1))
        def _():
            edge1_copy(source, 0 if source else 1).wait_recv()

        @pl.when(me == source)
        def _():
            edge1_own(source).wait()

    q_of = iota((tokens, tokens), 0)
    i_of = iota((tokens, tokens), 1)
    order = one_hot(i_of == (q_of % full) * block + q_of // full)
    edge_order = one_hot(
        (iota((EDGE, edge1.shape[0] * edge), 1) == iota((EDGE, edge1.shape[0] * edge), 0) * edge)
        & (iota((EDGE, edge1.shape[0] * edge), 0) < taps - 1)
    )
    u_ref[0:tokens, :] = dot(order, r1[...].reshape(tokens, width)).astype(BF16)
    u_ref[tokens : tokens + EDGE, :] = dot(
        edge_order, edge1[...].reshape(edge1.shape[0] * edge, width)
    ).astype(BF16)

    weights_in.wait()

    def layer_out(layer, backward, sent, gathered, sends, recvs):
        base = 0 if backward else EDGE
        normed = rms(u_ref[...].astype(F32), norm_gain[layer : layer + 1, :]).astype(BF16)
        x_ref[...] = dot(normed, in_w[layer, :, inner:]).astype(BF16).astype(F32)
        z_ref[...] = dot(normed[base : base + tokens], in_w[layer, :, :inner]).astype(BF16)
        proj = dot(normed, state_weight[layer]).astype(BF16).astype(F32)
        p_ref[:, 0 : proj.shape[1]] = proj

        def shifted(ref, start, size, k):
            begin = start + (taps - 1 - k if backward else EDGE - (taps - 1) + k)
            return ref[begin : begin + size, :]

        lower = iota((GROUP, GROUP), 0) >= iota((GROUP, GROUP), 1)
        upper = iota((GROUP, GROUP), 0) <= iota((GROUP, GROUP), 1)
        allowed = upper if backward else lower
        summing = one_hot(allowed)
        narrow = iota((GROUP, lanes), 1)
        even = iota((GROUP, lanes), 1) < HEADDIM
        skip = dot(
            jnp.broadcast_to(halves(small[layer, 7:8, :]), (16, 2 * lanes)), spread
        )[0:1]
        sequence = list(range(groups))[:: -1 if backward else 1]
        last_row = 0 if backward else GROUP - 1
        carried = None
        decay = None
        for g in sequence:
            start = g * GROUP
            conv_x = jnp.broadcast_to(conv_bias[layer : layer + 1, :inner], (GROUP, inner))
            conv_p = jnp.broadcast_to(small[layer, 4:5, :], (GROUP, lanes))
            for k in range(taps):
                conv_x = conv_x + conv_weight[layer, k : k + 1, :inner] * shifted(
                    x_ref, start, GROUP, k
                )
                conv_p = conv_p + small[layer, k : k + 1, :] * shifted(p_ref, start, GROUP, k)
            xc = silu(conv_x).astype(BF16)
            bc = silu(conv_p)
            b_part = jnp.where(narrow < STATE, bc, 0.0)
            c_part = jnp.where(narrow < STATE, pltpu.roll(bc, lanes - STATE, 1), 0.0)
            b_low = b_part.astype(BF16)
            c_low = c_part.astype(BF16)
            c_ref[start : start + GROUP, :] = c_low
            raw = pltpu.roll(
                p_ref[base + start : base + start + GROUP, :], lanes - 2 * STATE, 1
            )
            raw = raw + small[layer, 5:6, :]
            step = jnp.maximum(raw, 0.0) + jnp.log1p(jnp.exp(-jnp.abs(raw)))
            step = jnp.where(narrow < HEADS, step, 0.0)
            rate = -step * jnp.exp(small[layer, 6:7, :])
            both = dot(summing, halves(rate))
            cum = both[:, :lanes] + both[:, lanes:]
            cum_rows = jnp.transpose(cum)
            grown = dot(halves(jnp.where(narrow < HEADS, jnp.exp(cum), 0.0)), spread)
            grow_ref[start : start + GROUP, :] = grown
            last = cum[last_row : last_row + 1, :]
            tail = dot(halves(jnp.exp(last - cum) * step), spread)
            stepped = dot(halves(step), spread)
            scores = lax.dot_general(
                c_low, b_low, (((1,), (1,)), ((), ())), preferred_element_type=F32
            )
            scores = jnp.where(allowed, scores, 0.0)
            xf = xc.astype(F32)
            weighted = (xf * tail).astype(BF16)
            local = dot(jnp.transpose(b_part)[0:STATE, :].astype(BF16), weighted)
            local_ref[g] = local
            grown_last = grown[last_row : last_row + 1, :]
            carried = local if carried is None else grown_last * carried + local
            decay = grown_last if decay is None else decay * grown_last
            step_x = xf * stepped
            for pair in range(HEADS // 2):
                at = slice(pair * lanes, (pair + 1) * lanes)
                xp = step_x[:, at]
                total = None
                for side in range(2):
                    h = 2 * pair + side
                    diff = jnp.minimum(cum[:, h : h + 1] - cum_rows[h : h + 1, :], 0.0)
                    weights = (scores * jnp.exp(diff)).astype(BF16)
                    masked = jnp.where(even if side == 0 else ~even, xp, 0.0).astype(BF16)
                    term = dot(weights, masked)
                    total = term if total is None else total + term
                y_ref[start : start + GROUP, at] = total + skip[:, at] * xf[:, at]

        sent[0:STATE, :] = carried.astype(BF16)
        decay_high = decay.astype(BF16).astype(F32)
        decay_rows = jnp.where(
            iota((STATE, inner), 0) == 0,
            decay_high,
            jnp.where(iota((STATE, inner), 0) == 1, decay - decay_high, 0.0),
        )
        sent[STATE : 2 * STATE, :] = decay_rows.astype(BF16)

        def state_copy(source, j):
            return remote(sent, gathered.at[source], sends.at[j], recvs.at[source], j)

        for j in range(n):

            @pl.when((me > j) if backward else (me < j))
            def _():
                state_copy(me, j).start()

        arrive[...] = jnp.zeros_like(arrive)
        for i in list(range(n))[:: -1 if backward else 1]:

            @pl.when((me < i) if backward else (me > i))
            def _():
                state_copy(i, (i + 1) % n).wait_recv()
                factor = jnp.sum(gathered[i, STATE : 2 * STATE, :].astype(F32), 0, keepdims=True)
                arrive[...] = factor * arrive[...] + gathered[i, 0:STATE, :].astype(F32)

        for j in range(n):

            @pl.when((me > j) if backward else (me < j))
            def _():
                state_copy(me, j).wait_send()

        state = arrive[...]
        results = [None] * groups
        for g in sequence:
            start = g * GROUP
            grown = grow_ref[start : start + GROUP, :]
            inter = dot(c_ref[start : start + GROUP, 0:STATE], state.astype(BF16))
            y = y_ref[start : start + GROUP, :] + grown * inter
            state = grown[last_row : last_row + 1, :] * state + local_ref[g]
            gated = y * silu(z_ref[start : start + GROUP, :].astype(F32))
            mixed = rms(gated, out_gain[layer : layer + 1, :]).astype(BF16)
            token = u_ref[base + start : base + start + GROUP, :].astype(F32)
            results[g] = (token + dot(mixed, out_w[layer])).astype(BF16)
        return jnp.concatenate(results, axis=0)

    weights_out.wait()
    after = layer_out(0, True, send0, gather0, g0s, g0r)
    back = one_hot(i_of == (q_of % block) * full + q_of // block)
    o1[...] = dot(back, after).astype(BF16).reshape(full, block, width)

    second_copies = []
    for k in range(1, n):
        to = lax.rem(me + k, n)
        copy = remote(
            o1.at[at_rows(to)], r2.at[:, at_cols(me), :], s2.at[k - 1], v2.at[k - 1], to
        )
        copy.start()
        second_copies.append(copy)
    own2 = pltpu.make_async_copy(o1.at[at_rows(me)], r2.at[:, at_cols(me), :], l_sem.at[2])
    own2.start()

    def edge2_copy(j):
        return remote(
            o1.at[rows * j - 1, pl.ds(block - edge, edge), :], edge2, e2s.at[j], e2r, j
        )

    edge2_own = pltpu.make_async_copy(
        o1.at[rows * (n - 1) - 1, pl.ds(block - edge, edge), :], edge2, l_sem.at[3]
    )

    @pl.when(me == n - 1)
    def _():
        for j in range(1, n - 1):
            edge2_copy(j).start()
        edge2_own.start()

    own2.wait()
    for copy in second_copies:
        copy.wait_recv()

    @pl.when((me > 0) & (me < n - 1))
    def _():
        edge2_copy(1).wait_recv()

    @pl.when(me == n - 1)
    def _():
        edge2_own.wait()

    if edge < EDGE:
        u_ref[0 : EDGE - edge, :] = jnp.zeros((EDGE - edge, width), BF16)
    u_ref[EDGE - edge : EDGE, :] = edge2[...]
    u_ref[EDGE : EDGE + tokens, :] = r2[...].reshape(tokens, width)
    out[...] = layer_out(1, False, send1, gather1, g1s, g1r).reshape(rows, cols, width)

    for copy in first_copies:
        copy.wait_send()
    for copy in second_copies:
        copy.wait_send()
    for source in range(sources):

        @pl.when(me == source)
        def _():
            for j in range(n - 1):
                if j != source:
                    edge1_copy(source, j).wait_send()

    @pl.when(me == n - 1)
    def _():
        for j in range(1, n - 1):
            edge2_copy(j).wait_send()


def on_device(n, *arrays):
    slide, in_weight, out_weight = arrays[0], arrays[2], arrays[10]
    rows, cols, width = slide.shape
    full, block, tokens = rows * n, cols // n, rows * cols
    inner = in_weight.shape[2] // 2
    edge = min(EDGE, block)
    sources = -(-(arrays[4].shape[1] - 1) // rows)
    vmem = pl.BlockSpec(memory_space=pltpu.VMEM)
    hbm = pl.BlockSpec(memory_space=pl.ANY)
    dma = pltpu.SemaphoreType.DMA
    return pl.pallas_call(
        functools.partial(kernel, n),
        out_shape=jax.ShapeDtypeStruct((rows, cols, width), BF16),
        in_specs=[hbm, vmem, hbm] + [vmem] * 7 + [hbm],
        out_specs=vmem,
        scratch_shapes=[
            pltpu.VMEM(in_weight.shape, BF16),
            pltpu.VMEM(out_weight.shape, BF16),
            pltpu.VMEM((full, block, width), BF16),
            pltpu.VMEM((sources * rows, edge, width), BF16),
            pltpu.VMEM((full, block, width), BF16),
            pltpu.VMEM((rows, cols, width), BF16),
            pltpu.VMEM((edge, width), BF16),
            pltpu.VMEM((tokens + EDGE, width), BF16),
            pltpu.VMEM((tokens + EDGE, inner), F32),
            pltpu.VMEM((tokens + EDGE, 128), F32),
            pltpu.VMEM((2, 8, 128), F32),
            pltpu.VMEM((tokens, inner), BF16),
            pltpu.VMEM((tokens, inner), F32),
            pltpu.VMEM((tokens, inner), F32),
            pltpu.VMEM((tokens, 128), BF16),
            pltpu.VMEM((tokens // GROUP, STATE, inner), F32),
            pltpu.VMEM((2 * STATE, inner), BF16),
            pltpu.VMEM((2 * STATE, inner), BF16),
            pltpu.VMEM((n, 2 * STATE, inner), BF16),
            pltpu.VMEM((n, 2 * STATE, inner), BF16),
            pltpu.VMEM((STATE, inner), F32),
            dma((2,)),
            dma((4,)),
            dma((n,)),
            dma((n,)),
            dma((n,)),
            dma((n,)),
            dma((n,)),
            dma((n,)),
            dma((n,)),
            dma,
            dma((n,)),
            dma((n,)),
            dma((n,)),
            dma((n,)),
        ],
        compiler_params=pltpu.CompilerParams(
            collective_id=0, has_side_effects=True, vmem_limit_bytes=60 * 1024 * 1024
        ),
    )(*arrays)


def solution(mesh):
    placed = (P(("dp", "seq"), None, None),) + (P(),) * 10
    return jax.shard_map(
        functools.partial(on_device, mesh.shape["seq"]),
        mesh=mesh,
        in_specs=placed,
        out_specs=P(("dp", "seq"), None, None),
        check_vma=False,
    )
```

time: 140 us -> 49.3 us (0.35)
  blocking collectives: 48.3 us -> 0 us
  Pallas kernels: 0 us -> 45.5 us
  local copies, waits for them, and re-layouts: 28.6 us -> 3.5 us
  matrix products: 17.9 us -> 0 us
  starting transfers between devices: 17.7 us -> 0 us
  other arithmetic: 13.7 us -> 0 us
  waiting for transfers between devices: 9.95 us -> 0 us
  between operations: 1.55 us -> 0.01 us
    pallas_call x0 -> x1, Pallas kernels: none -> 45.5 us  [on_device(): pl.pallas_call(functools.partial(kernel, n), out_shape=jax.ShapeDtypeStru...]
    unnamed x2 -> x0, blocking collectives: 26.5 us -> none
    all_gather x2 -> x0, blocking collectives: 21.8 us -> none  [entering_2(): lax.all_gather(a.astype(kind), axis)]
    dot_general x20 -> x0, matrix products: 17.9 us -> none  [the longest x2 4.51 us: mixer(): jnp.dot(normed, in_weight[layer], preferred_element_type=jnp.float32)]
    all_to_all x2 -> x0, waiting for transfers between devices: 9.94 us -> none  [the longest x1 8.22 us: on_device(): lax.all_to_all(row_grid, 'seq', split_axis=0, concat_axis=1, tiled=True)]
    ppermute x4 -> x0, starting transfers between devices: 8.94 us -> none  [passed_along(): lax.ppermute(value, axis, [(source, source + steps) for source in range(f...]
    all_to_all x2 -> x0, starting transfers between devices: 8.78 us -> none  [the longest x1 5.2 us: on_device(): lax.all_to_all(flipped, 'seq', split_axis=1, concat_axis=0, tiled=True)]
    reduce_sum x6 -> x0, other arithmetic: 5.95 us -> none  [the longest x4 3.99 us: rms_scaled(): jnp.mean(values * values, axis=-1, keepdims=True) + epsilon]
  transfers between devices with their start and end apart: 6 -> 0, of which waited for: 2 -> 0; matrix products, arithmetic and copies ran while one was open for 6% -> 0% of each run, Pallas kernels for 0% -> 0%
where the time goes in v1:
time: 49.3 us; the launch traced here: 49 us
  Pallas kernels  45.5 us (92%)
  local copies, waits for them, and re-layouts  3.5 us (7%)
    pallas_call x1, Pallas kernels, on_device(): pl.pallas_call(functools.partial(kernel, n), out_shape=jax.ShapeDtypeStru...  45.5 us
    unnamed x2, local copies, waits for them, and re-layouts  3.5 us

profile of v1, /device:TPU:0, one launch (start us, length us, event | category | flops | bytes accessed | tf_op | source)
XLA Modules:
  0.0 49.0 jit_solution(13118683066692152469)
XLA Ops:
  0.0 1.7 %copy.12.state_weight = bf16[2,384,44]{2,1,0:T(8,128)(2,1)} copy(bf16[2,384,44]{1,0,2:T(2,128)(2,1)} %param.14) | data formatting | bytes 135168 | tf_op args[3]
  1.7 45.5 %shard_map.109 = bf16[2,256,384]{2,1,0:T(8,128)(2,1)} custom-call(bf16[2,256,384]{2,1,0:T(8,128)(2,1)} %slide.1, f32[2,384]{1,0:T(2,128)} %norm_gain.1, bf16[2,384,1536]{2,1,0:T(8,128)(2,1)} %in_hbm.1, bf16[2,384,44]{2,1,0:T(8,128)(2,1)} %copy.12.state_weight, f32[2,4,800]{2,1,0:T(4,128)} %conv_weight.1, f32[2,800]{1,0:T(2,128)} %conv_bias.1, ...), custom_call_target="tpu_custom_call" | custom-call | tf_op jit(solution)/shard_map/pallas_call | solution.py:425
  47.3 1.8 %copy.14 = bf16[2,256,384]{2,1,0:T(8,128)(2,1)} copy(bf16[2,256,384]{2,1,0:T(8,128)(2,1)} %shard_map.109) | data formatting | bytes 786432

commit v2 on v1

--- a/solution.py
+++ b/solution.py
@@ -10,7 +10,7 @@
 HEADS = 12
 HEADDIM = 64
 STATE = 16
-GROUP = 256
+GROUP = 128
 EDGE = 16
 EPS = 1e-05
 MESH = pl.DeviceIdType.MESH
@@ -74,6 +74,14 @@
     y_ref,
     grow_ref,
     c_ref,
+    xc_ref,
+    step_ref,
+    cum_ref,
+    row_ref,
+    score_ref,
+    order_ref,
+    back_ref,
+    normed_ref,
     local_ref,
     send0,
     send1,
@@ -188,7 +196,12 @@
 
     lanes = 128
     spread_row = iota((2 * lanes, inner), 0)
-    spread = one_hot((spread_row % lanes) == (iota((2 * lanes, inner), 1) // HEADDIM))
+    spread = one_hot(jnp.bitwise_and(spread_row, lanes - 1) == iota((1, inner), 1) // HEADDIM)
+
+    line = iota((tokens, tokens), 0)
+    lane_at = iota((1, tokens), 1)
+    order_ref[...] = one_hot(line == (lane_at % block) * full + lane_at // block)
+    back_ref[...] = one_hot(line == (lane_at % full) * block + lane_at // full)
 
     own.wait()
     for copy in first_copies:
@@ -203,14 +216,11 @@
         def _():
             edge1_own(source).wait()
 
-    q_of = iota((tokens, tokens), 0)
-    i_of = iota((tokens, tokens), 1)
-    order = one_hot(i_of == (q_of % full) * block + q_of // full)
     edge_order = one_hot(
         (iota((EDGE, edge1.shape[0] * edge), 1) == iota((EDGE, edge1.shape[0] * edge), 0) * edge)
         & (iota((EDGE, edge1.shape[0] * edge), 0) < taps - 1)
     )
-    u_ref[0:tokens, :] = dot(order, r1[...].reshape(tokens, width)).astype(BF16)
+    u_ref[0:tokens, :] = dot(order_ref[...], r1[...].reshape(tokens, width)).astype(BF16)
     u_ref[tokens : tokens + EDGE, :] = dot(
         edge_order, edge1[...].reshape(edge1.shape[0] * edge, width)
     ).astype(BF16)
@@ -221,8 +231,11 @@
         base = 0 if backward else EDGE
         normed = rms(u_ref[...].astype(F32), norm_gain[layer : layer + 1, :]).astype(BF16)
         x_ref[...] = dot(normed, in_w[layer, :, inner:]).astype(BF16).astype(F32)
-        z_ref[...] = dot(normed[base : base + tokens], in_w[layer, :, :inner]).astype(BF16)
-        proj = dot(normed, state_weight[layer]).astype(BF16).astype(F32)
+        normed_ref[...] = normed
+        proj = lax.dot_general(
+            normed, state_weight[layer], (((1,), (1,)), ((), ())), preferred_element_type=F32
+        )
+        proj = proj.astype(BF16).astype(F32)
         p_ref[:, 0 : proj.shape[1]] = proj
 
         def shifted(ref, start, size, k):
@@ -284,19 +297,11 @@
             grown_last = grown[last_row : last_row + 1, :]
             carried = local if carried is None else grown_last * carried + local
             decay = grown_last if decay is None else decay * grown_last
-            step_x = xf * stepped
-            for pair in range(HEADS // 2):
-                at = slice(pair * lanes, (pair + 1) * lanes)
-                xp = step_x[:, at]
-                total = None
-                for side in range(2):
-                    h = 2 * pair + side
-                    diff = jnp.minimum(cum[:, h : h + 1] - cum_rows[h : h + 1, :], 0.0)
-                    weights = (scores * jnp.exp(diff)).astype(BF16)
-                    masked = jnp.where(even if side == 0 else ~even, xp, 0.0).astype(BF16)
-                    term = dot(weights, masked)
-                    total = term if total is None else total + term
-                y_ref[start : start + GROUP, at] = total + skip[:, at] * xf[:, at]
+            step_ref[start : start + GROUP, :] = (xf * stepped).astype(BF16)
+            xc_ref[start : start + GROUP, :] = xc
+            cum_ref[start : start + GROUP, :] = cum
+            row_ref[g] = cum_rows[0:16, :]
+            score_ref[start : start + GROUP, :] = scores
 
         sent[0:STATE, :] = carried.astype(BF16)
         decay_high = decay.astype(BF16).astype(F32)
@@ -315,6 +320,22 @@
             @pl.when((me > j) if backward else (me < j))
             def _():
                 state_copy(me, j).start()
+
+        z_ref[...] = dot(normed_ref[base : base + tokens, :], in_w[layer, :, :inner]).astype(BF16)
+        for g in sequence:
+            here = slice(g * GROUP, (g + 1) * GROUP)
+            scores = score_ref[here, :]
+            for pair in range(HEADS // 2):
+                at = slice(pair * lanes, (pair + 1) * lanes)
+                xp = step_ref[here, at]
+                total = skip[:, at] * xc_ref[here, at].astype(F32)
+                for side in range(2):
+                    h = 2 * pair + side
+                    diff = cum_ref[here, h : h + 1] - row_ref[g, h : h + 1, :]
+                    weights = (scores * jnp.exp(jnp.minimum(diff, 0.0))).astype(BF16)
+                    kept = even if side == 0 else ~even
+                    total = total + dot(weights, jnp.where(kept, xp, jnp.zeros_like(xp)))
+                y_ref[here, at] = total
 
         arrive[...] = jnp.zeros_like(arrive)
         for i in list(range(n))[:: -1 if backward else 1]:
@@ -347,8 +368,7 @@
 
     weights_out.wait()
     after = layer_out(0, True, send0, gather0, g0s, g0r)
-    back = one_hot(i_of == (q_of % block) * full + q_of // block)
-    o1[...] = dot(back, after).astype(BF16).reshape(full, block, width)
+    o1[...] = dot(back_ref[...], after).astype(BF16).reshape(full, block, width)
 
     second_copies = []
     for k in range(1, n):
@@ -443,6 +463,14 @@
             pltpu.VMEM((tokens, inner), F32),
             pltpu.VMEM((tokens, inner), F32),
             pltpu.VMEM((tokens, 128), BF16),
+            pltpu.VMEM((tokens, inner), BF16),
+            pltpu.VMEM((tokens, inner), BF16),
+            pltpu.VMEM((tokens, 128), F32),
+            pltpu.VMEM((tokens // GROUP, 16, GROUP), F32),
+            pltpu.VMEM((tokens, GROUP), F32),
+            pltpu.VMEM((tokens, tokens), BF16),
+            pltpu.VMEM((tokens, tokens), BF16),
+            pltpu.VMEM((tokens + EDGE, width), BF16),
             pltpu.VMEM((tokens // GROUP, STATE, inner), F32),
             pltpu.VMEM((2 * STATE, inner), BF16),
             pltpu.VMEM((2 * STATE, inner), BF16),
@@ -467,7 +495,7 @@
         compiler_params=pltpu.CompilerParams(
             collective_id=0, has_side_effects=True, vmem_limit_bytes=60 * 1024 * 1024
         ),
-    )(*arrays)
+    )(*arrays[:3], jnp.swapaxes(arrays[3], 1, 2), *arrays[4:])
 
 
 def solution(mesh):

time: 49.3 us -> 45.9 us (0.931)
  Pallas kernels: 45.5 us -> 42.3 us
    pallas_call x1, Pallas kernels: 45.5 us -> 42.3 us  [on_device(): pl.pallas_call(functools.partial(kernel, n), out_shape=jax.ShapeDtypeStru...]
where the time goes in v2:
time: 45.9 us; the launch traced here: 45.6 us
  Pallas kernels  42.3 us (92%)
  local copies, waits for them, and re-layouts  3.31 us (7%)
    pallas_call x1, Pallas kernels, on_device(): pl.pallas_call(functools.partial(kernel, n), out_shape=jax.ShapeDtypeStru...  42.3 us
    unnamed x2, local copies, waits for them, and re-layouts  3.31 us

profile of v2, /device:TPU:0, one launch (start us, length us, event | category | flops | bytes accessed | tf_op | source)
XLA Modules:
  0.0 45.6 jit_solution(7674644051663181593)
XLA Ops:
  0.0 1.5 %copy.14 = bf16[2,384,44]{1,2,0:T(8,128)(2,1)} copy(bf16[2,384,44]{1,0,2:T(2,128)(2,1)} %param.14) | data formatting | bytes 135168 | tf_op args[3]
  1.5 42.3 %shard_map.109 = bf16[2,256,384]{2,1,0:T(8,128)(2,1)} custom-call(bf16[2,256,384]{2,1,0:T(8,128)(2,1)} %slide.1, f32[2,384]{1,0:T(2,128)} %norm_gain.1, bf16[2,384,1536]{2,1,0:T(8,128)(2,1)} %in_hbm.1, bf16[2,44,384]{2,1,0:T(8,128)(2,1)} %bitcast.3, f32[2,4,800]{2,1,0:T(4,128)} %conv_weight.1, f32[2,800]{1,0:T(2,128)} %conv_bias.1, f32[2,12]{1,0:T(2,128)} %step_bias.1, ...), custom_call_target="tpu_custom_call" | custom-call | tf_op jit(solution)/shard_map/pallas_call | solution.py:445
  43.9 1.8 %copy.16 = bf16[2,256,384]{2,1,0:T(8,128)(2,1)} copy(bf16[2,256,384]{2,1,0:T(8,128)(2,1)} %shard_map.109) | data formatting | bytes 786432
